TPU v7x, 32 devices: a whole 2x2x4 slice. The times are simulated.
32 devices in a mesh: groups: 2 (over y), blk: 16 (over z, x, core).
Axes of the slice: x: 2, y: 2, z: 4, core: 2. Of those that a mesh axis runs over, the one named last changes fastest.
Arguments:
- query_hidden: bfloat16 [512, 32, 768], P(('groups', 'blk')), parts along dimension 0, may hold values from -6 to 6
- passage_hidden: bfloat16 [256, 180, 768], P(('groups', 'blk')), parts along dimension 0, may hold values from -6 to 6
- projection: bfloat16 [768, 128], replicated, may hold values from -0.21875 to 0.21875
- teacher_rows: float32 [512, 32], P(('groups', 'blk')), parts along dimension 0, may hold values from -12 to 12
- teacher_pos: int32 [512], P(('groups', 'blk')), parts along dimension 0, may hold values from 0 to 255, each once
- neg_count: int32 [512], P(('groups', 'blk')), parts along dimension 0, may hold values from 8 to 32
- pass_len: int32 [256], P(('groups', 'blk')), parts along dimension 0, may hold values from 19 to 180
Outputs:
- loss: float32 [512], P(('groups', 'blk')), parts along dimension 0
- grad_w: float32 [1536, 128], P(('groups', 'blk')), parts along dimension 0
There are 2 independent parts, one for each index of `groups`. A program takes and returns all parts, laid end to end along the dimension named above; an argument that names none is the same for every part. Nothing has to cross between parts.
Inputs may be any that keep to these rules, and one draw needn't show every extreme that they name: A permutation: the teacher scores of query q are stored as row teacher_pos[q] of teacher_rows.
All inputs are finite; a program needn't handle non-finite values.
Results may differ from a plain program's by a relative error of at most 0.0073.
Values may be sent and summed in bfloat16 or wider, within the bound.
A program may use at most 128 MiB of HBM per device.

v0:
```python
import jax
import jax.numpy as jnp
from jax import lax
from jax.sharding import PartitionSpec as P

CYCLE = 4
smoothing_heat_factor = 0.05
epsilon = 1e-06


def shifted(value, axis, steps):
    count = lax.axis_size(axis)
    pairs = [(source, (source + steps) % count) for source in range(count)]
    return lax.ppermute(value, axis, pairs)


def normalize(raw):
    length = jnp.sqrt(jnp.sum(raw * raw, axis=1, keepdims=True) + epsilon)
    return (raw / length, length)


def token_terms(query_flat, passage_flat, lengths):
    count = lengths.shape[0]
    token_affinity_table = lax.dot_general(
        query_flat, passage_flat, (((1,), (1,)), ((), ())), preferred_element_type=jnp.float32
    )
    token_affinity_table = token_affinity_table.reshape(query_flat.shape[0], count, -1)
    pairwise_dot_entries = (
        jnp.arange(token_affinity_table.shape[2], dtype=jnp.int32)[None, :] < lengths[:, None]
    )
    natural_power_entries = jnp.where(
        pairwise_dot_entries[None], jnp.exp(token_affinity_table / smoothing_heat_factor), 0.0
    )
    return (natural_power_entries, jnp.sum(natural_power_entries, axis=2))


def soft_scores(query_flat, passage_flat, lengths, query_matrix):
    natural_power_entries, power_totals_row = token_terms(query_flat, passage_flat, lengths)
    smooth_peak_values = smoothing_heat_factor * jnp.log(power_totals_row)
    return jnp.sum(smooth_peak_values.reshape(query_matrix, -1, lengths.shape[0]), axis=1)


def score_grads(query_flat, passage_flat, lengths, score_grad):
    natural_power_entries, power_totals_row = token_terms(query_flat, passage_flat, lengths)
    rows = query_flat.shape[0]
    query_matrix, count = score_grad.shape
    scale = (score_grad[:, None, :] / power_totals_row.reshape(query_matrix, -1, count)).reshape(
        rows, count
    )
    weights = (natural_power_entries * scale[:, :, None]).reshape(rows, -1).astype(jnp.bfloat16)
    query_grad = jnp.dot(weights, passage_flat, preferred_element_type=jnp.float32)
    passage_grad = lax.dot_general(
        weights, query_flat, (((0,), (0,)), ((), ())), preferred_element_type=jnp.float32
    )
    return (query_grad, passage_grad)


def kl_terms(student, teacher, counts):
    valid = jnp.arange(student.shape[1], dtype=jnp.int32)[None, :] < counts[:, None]
    student_exp = jnp.where(valid, jnp.exp(student), 0.0)
    student_total = jnp.sum(student_exp, axis=1, keepdims=True)
    teacher_exp = jnp.where(valid, jnp.exp(teacher), 0.0)
    teacher_total = jnp.sum(teacher_exp, axis=1, keepdims=True)
    student_prob = student_exp / student_total
    teacher_prob = teacher_exp / teacher_total
    gap = teacher - jnp.log(teacher_total) - (student - jnp.log(student_total))
    loss = jnp.sum(jnp.where(valid, teacher_prob * gap, 0.0), axis=1)
    return (loss, student_prob - teacher_prob)


def raw_grad(unit, length, grad):
    return ((grad - unit * jnp.sum(unit * grad, axis=1, keepdims=True)) / length).astype(
        jnp.bfloat16
    )


def per_device(
    query_hidden, passage_hidden, projection, teacher_rows, teacher_pos, neg_count, pass_len
):
    query_matrix = query_hidden.shape[0]
    query_tokens = query_hidden.shape[1]
    width = query_hidden.shape[2]
    passages = passage_hidden.shape[0]
    passage_tokens = passage_hidden.shape[1]
    query_flat = query_hidden.reshape(query_matrix * query_tokens, width)
    passage_flat = passage_hidden.reshape(passages * passage_tokens, width)
    query_unit, query_length = normalize(
        jnp.dot(query_flat, projection, preferred_element_type=jnp.float32)
    )
    passage_unit, passage_length = normalize(
        jnp.dot(passage_flat, projection, preferred_element_type=jnp.float32)
    )
    query_outgoing = query_unit.astype(jnp.bfloat16)
    passage_send = passage_unit.astype(jnp.bfloat16)
    stored = lax.all_gather(teacher_rows, "blk", axis=0, tiled=True)
    teacher = jnp.take(stored, teacher_pos, axis=0)
    score_parts = []
    held = []
    current = query_outgoing
    for offset in range(CYCLE):
        if offset > 0:
            current = shifted(current, "blk", 1)
        held.append(current)
        scored = soft_scores(current, passage_send, pass_len, query_matrix)
        if offset > 0:
            scored = shifted(scored, "blk", -offset)
        score_parts.append(scored)
    student = jnp.concatenate(score_parts, axis=1)
    loss, score_grad = kl_terms(student, teacher, neg_count)
    query_total = jnp.zeros(query_unit.shape, jnp.float32)
    passage_total = jnp.zeros(passage_unit.shape, jnp.float32)
    for offset in range(CYCLE):
        portion_derivative = score_grad[:, offset * passages : (offset + 1) * passages]
        if offset > 0:
            portion_derivative = shifted(portion_derivative, "blk", offset)
        query_part, passage_part = score_grads(
            held[offset], passage_send, pass_len, portion_derivative
        )
        passage_total = passage_total + passage_part
        if offset > 0:
            query_part = shifted(query_part, "blk", -offset)
        query_total = query_total + query_part
    query_raw = raw_grad(query_unit, query_length, query_total)
    document_unprojected = raw_grad(passage_unit, passage_length, passage_total)
    contract = (((0,), (0,)), ((), ()))
    term = lax.dot_general(query_flat, query_raw, contract, preferred_element_type=jnp.float32)
    grad_w = lax.psum_scatter(
        term
        + lax.dot_general(
            passage_flat, document_unprojected, contract, preferred_element_type=jnp.float32
        ),
        "blk",
        scatter_dimension=0,
        tiled=True,
    )
    return (loss, grad_w)


def solution(mesh):
    return jax.shard_map(
        per_device,
        mesh=mesh,
        in_specs=(
            P(("groups", "blk"), None, None),
            P(("groups", "blk"), None, None),
            P(),
            P(("groups", "blk"), None),
            P(("groups", "blk")),
            P(("groups", "blk")),
            P(("groups", "blk")),
        ),
        out_specs=(P(("groups", "blk")), P(("groups", "blk"), None)),
        check_vma=False,
    )
```

profile of v0, /device:TPU:0, one launch (start us, length us, event | category | flops | bytes accessed | tf_op | source)
XLA Modules:
  0.0 242.0 jit_solution(9073984573945769077)
XLA Ops:
  7.2 1.1 copy-done
  8.3 1.3 multiply_reduce_fusion.3
  10.9 1.2 compare_and_fusion
  12.8 1.3 iota_compare_fusion
  14.1 3.4 %copy.26 = bf16[8,180,768]{2,1,0:T(8,128)(2,1)} copy(bf16[8,180,768]{2,0,1:T(8,128)(2,1)} %param.8) | data formatting | bytes 4423680 | tf_op args[1]
  17.5 2.6 %reshape.162 = bf16[1440,768]{1,0:T(8,128)(2,1)S(1)} reshape(bf16[8,180,768]{2,1,0:T(8,128)(2,1)} %copy.26) | data formatting | bytes 4423680 | tf_op jit(solution)/shard_map/reshape | solution.py:86
  20.1 0.9 multiply_reduce_fusion.1
  21.0 0.8 copy-done.1
  22.1 2.1 fusion
  24.5 3.1 %exp.40 = f32[512,8,180]{0,2,1:T(8,128)} reshape(f32[512,1440]{0,1:T(8,128)} %fusion) | data formatting | bytes 5898240 | tf_op jit(solution)/shard_map/exp | solution.py:32
  27.6 24.4 %all_gather.3 = f32[256,32]{1,0:T(8,128)} all-gather(f32[16,32]{1,0:T(8,128)S(1)} %copy-done.11), channel_id=1, replica_groups=mesh['groups'=2,'blk'=16] {'blk'}, dimensions={0}, use_global_device_ids=true | all-gather | bytes 34816 | tf_op jit(solution)/shard_map/all_gather | solution.py:95
  52.9 3.1 %fusion.1 = f32[512,1440]{0,1:T(8,128)} fusion(bf16[1440,128]{1,0:T(8,128)(2,1)S(1)} %fusion.16, bf16[512,128]{0,1:T(8,128)(2,1)} %collective-permute-done), kind=kOutput, calls=%fused_computation.6 | convolution fusion | flops 189480960 | bytes 3448832 | tf_op jit(solution)/shard_map/dot_general | solution.py:24
  55.9 3.1 %exp.42 = f32[512,8,180]{0,2,1:T(8,128)} reshape(f32[512,1440]{0,1:T(8,128)} %fusion.1) | data formatting | bytes 5898240 | tf_op jit(solution)/shard_map/exp | solution.py:32
  59.1 0.9 collective-permute-done.2
  59.9 3.1 %fusion.2 = f32[512,1440]{0,1:T(8,128)} fusion(bf16[1440,128]{1,0:T(8,128)(2,1)S(1)} %fusion.16, bf16[512,128]{0,1:T(8,128)(2,1)} %collective-permute-done.2), kind=kOutput, calls=%fused_computation.7 | convolution fusion | flops 189480960 | bytes 3448832 | tf_op jit(solution)/shard_map/dot_general | solution.py:24
  63.0 3.2 %exp.44 = f32[512,8,180]{0,2,1:T(8,128)} reshape(f32[512,1440]{0,1:T(8,128)} %fusion.2) | data formatting | bytes 5898240 | tf_op jit(solution)/shard_map/exp | solution.py:32
  66.2 1.1 collective-permute-done.4
  67.3 3.0 %fusion.3 = f32[512,1440]{0,1:T(8,128)} fusion(bf16[1440,128]{1,0:T(8,128)(2,1)S(1)} %fusion.16, bf16[512,128]{0,1:T(8,128)(2,1)} %collective-permute-done.4), kind=kOutput, calls=%fused_computation.8 | convolution fusion | flops 189480960 | bytes 3448832 | tf_op jit(solution)/shard_map/dot_general | solution.py:24
  70.4 3.1 %exp.46 = f32[512,8,180]{0,2,1:T(8,128)} reshape(f32[512,1440]{0,1:T(8,128)} %fusion.3) | data formatting | bytes 5898240 | tf_op jit(solution)/shard_map/exp | solution.py:32
  73.5 5.7 %select_reduce_fusion.3 = (f32[512,8]{0,1:T(8,128)}, f32[512,8]{0,1:T(8,128)S(1)}, f32[512,8]{0,1:T(8,128)S(1)}, f32[512,8]{0,1:T(8,128)S(1)}) fusion(f32[512,8,180]{0,2,1:T(8,128)} %exp.40, pred[8,180]{1,0:T(8,128)(4,1)} %iota_compare_fusion, f32[512,8,180]{0,2,1:T(8,128)} %exp.42, f32[512,8,180]{0,2,1:T(8,128)} %exp.44, f32[512,8,180]{0,2,1:T(8,128)} %exp.46), kind=kLoop, calls=%fused_computation.12 | loop fusion | flops 5881856 | bytes 11863456 | tf_op jit(solution)/shard_map/reduce_sum | solution.py:34
  79.9 1.4 mul.112
  81.3 1.5 reduce_sum.161
  82.8 1.3 copy.29
  84.1 1.3 log_multiply_fusion.2
  85.5 1.4 mul.108
  86.9 1.5 reduce_sum.157
  88.4 1.3 copy.27
  89.8 3.4 %collective-permute-start.1 = (f32[16,8]{1,0:T(8,128)}, f32[16,8]{1,0:T(8,128)}, u32[]{:S(2)}, u32[]{:S(2)}) collective-permute-start(f32[16,8]{1,0:T(8,128)} %copy.27), channel_id=1, source_target_pairs={{0,15},{1,0},{2,1},{3,2},{4,3},{5,4},{6,5},{7,6},{8,7},{9,8},{10,9... | collective-permute-start | bytes 1544 | tf_op jit(solution)/shard_map/ppermute | solution.py:14
  93.2 1.4 mul.110
  94.6 1.5 reduce_sum.159
  96.1 1.3 copy.28
  98.0 1.4 lt.39
  99.4 1.3 lt.42
  100.7 1.6 gather_fusion
  102.2 1.4 mul.106
  103.7 1.5 reduce_sum.155
  105.2 1.3 copy.30
  106.5 1.0 fusion.14
  107.5 1.4 divide_subtract_fusion
  110.4 3.5 %collective-permute-start.10 = (f32[16,8]{1,0:T(8,128)}, f32[16,8]{1,0:T(8,128)}, u32[]{:S(2)}, u32[]{:S(2)}) collective-permute-start(f32[16,8]{1,0:T(8,128)} %get-tuple-element.17), channel_id=1, source_target_pairs={{0,3},{1,4},{2,5},{3,6},{4,7},{5,8},{6,9},{7,10},{8,11},{9,12},{10... | collective-permute-start | bytes 1544 | tf_op jit(solution)/shard_map/ppermute | solution.py:14
  113.8 1.4 div.128
  115.2 1.5 div.129
  117.5 2.0 mul.114
  119.5 3.1 %mul.115 = f32[512,1440]{0,1:T(8,128)} reshape(f32[512,8,180]{0,2,1:T(8,128)} %mul.114) | data formatting | bytes 5898240 | tf_op jit(solution)/shard_map/mul | solution.py:50
  124.1 1.5 div.132
  125.6 1.3 div.133
  128.4 1.5 div.135
  132.1 1.5 div.138
  134.4 2.0 mul.123
  136.4 3.1 %mul.124 = f32[512,1440]{0,1:T(8,128)} reshape(f32[512,8,180]{0,2,1:T(8,128)} %mul.123) | data formatting | bytes 5898240 | tf_op jit(solution)/shard_map/mul | solution.py:50
  139.5 2.0 mul.120
  141.5 3.1 %mul.121 = f32[512,1440]{0,1:T(8,128)} reshape(f32[512,8,180]{0,2,1:T(8,128)} %mul.120) | data formatting | bytes 5898240 | tf_op jit(solution)/shard_map/mul | solution.py:50
  144.6 2.1 mul.117
  146.7 3.1 %mul.118 = f32[512,1440]{0,1:T(8,128)} reshape(f32[512,8,180]{0,2,1:T(8,128)} %mul.117) | data formatting | bytes 5898240 | tf_op jit(solution)/shard_map/mul | solution.py:50
  149.8 8.6 %multiply_convert_fusion = (bf16[512,1440]{0,1:T(8,128)(2,1)S(1)}, bf16[512,1440]{0,1:T(8,128)(2,1)S(1)}, bf16[512,1440]{0,1:T(8,128)(2,1)S(1)}, bf16[512,1440]{0,1:T(8,128)(2,1)S(1)}) fusion(f32[512,1440]{0,1:T(8,128)} %mul.124, f32[512,1440]{0,1:T(8,128)} %fusion.3, pred[1440]{0:T(1024)(128)(4,1)S(1)} %copy-done.12, f32[512,1440]{0,1:T(8,128)} %mul.118, ...), kind=kLoop, calls=%fused_computation.13 | loop fusion | flops 8847360 | bytes 29492640 | tf_op jit(solution)/shard_map/convert_element_type | solution.py:50
  159.7 4.8 %collective-permute-start.9 = (f32[512,128]{0,1:T(8,128)S(1)}, f32[512,128]{0,1:T(8,128)S(1)}, u32[]{:S(2)}, u32[]{:S(2)}) collective-permute-start(f32[512,128]{0,1:T(8,128)S(1)} %fusion.19), channel_id=1, source_target_pairs={{0,14},{1,15},{2,0},{3,1},{4,2},{5,3},{6,4},{7,5},{8,6},{9,7},{10,... | collective-permute-start | bytes 786440 | tf_op jit(solution)/shard_map/ppermute | solution.py:14
  165.0 1.5 convolution_add_fusion.2
  166.6 1.4 convolution_add_fusion.1
  168.0 1.6 multiply_reduce_fusion
  169.6 1.1 fusion.7
  171.2 3.2 %collective-permute-done.7 = f32[512,128]{0,1:T(8,128)S(1)} collective-permute-done((f32[512,128]{0,1:T(8,128)S(1)}, f32[512,128]{0,1:T(8,128)S(1)}, u32[]{:S(2)}, u32[]{:S(2)}) %collective-permute-start.7) | collective-permute-done | bytes 262176 | tf_op jit(solution)/shard_map/ppermute | solution.py:14
  174.5 2.8 %collective-permute-done.11 = f32[512,128]{0,1:T(8,128)S(1)} collective-permute-done((f32[512,128]{0,1:T(8,128)S(1)}, f32[512,128]{0,1:T(8,128)S(1)}, u32[]{:S(2)}, u32[]{:S(2)}) %collective-permute-start.11) | collective-permute-done | bytes 262176 | tf_op jit(solution)/shard_map/ppermute | solution.py:14
  178.0 0.9 copy.42
  179.0 56.2 %reduce-scatter.4.cloned.1.call-done = f32[48,128]{1,0:T(8,128)} async-done(((f32[768,128]{1,0:T(8,128)}), f32[48,128]{1,0:T(8,128)}) %reduce-scatter.4.cloned.1.call-update) | async-done | bytes 24592
  (74 shorter events, 15.6 us)
Async XLA Ops:
  7.2 1.1 copy-start
  7.2 228.0 %reduce-scatter.4.cloned.1.call-start = ((), (), s32[]{:S(2)}) async-start(), calls=%async_computation.1 | async-start | bytes 417792
  9.6 0.7 copy-start.3
  9.7 0.7 copy-start.9
  10.4 42.2 %collective-permute-start = (bf16[512,128]{0,1:T(8,128)(2,1)S(1)}, bf16[512,128]{0,1:T(8,128)(2,1)}, u32[]{:S(2)}, u32[]{:S(2)}) collective-permute-start(bf16[512,128]{0,1:T(8,128)(2,1)S(1)} %fusion.15), channel_id=1, source_target_pairs={{0,1},{1,2},{2,3},{3,4},{4,5},{5,6},{6,7},{7,8},{8,9},{9,10},{10,1... | collective-permute-start | bytes 393224 | tf_op jit(solution)/shard_map/ppermute | solution.py:14
  17.5 2.6 %copy-start.5 = (bf16[768,128]{1,0:T(8,128)(2,1)S(1)}, bf16[768,128]{1,0:T(8,128)(2,1)}, u32[]{:S(2)}) copy-start(bf16[768,128]{1,0:T(8,128)(2,1)} %param.9) | copy-start | bytes 589828
  21.0 0.9 copy-start.1
  21.0 3.3 %copy-start.13 = (s32[8]{0:T(128)S(1)}, s32[8]{0:T(128)}, u32[]{:S(2)}) copy-start(s32[8]{0:T(128)} %param.13) | copy-start | bytes 100
  21.0 1.1 copy-start.7
  24.4 3.1 %copy-start.11 = (f32[16,32]{1,0:T(8,128)S(1)}, f32[16,32]{1,0:T(8,128)}, u32[]{:S(2)}) copy-start(f32[16,32]{1,0:T(8,128)} %param.10) | copy-start | bytes 6148
  52.5 7.4 %collective-permute-start.2 = (bf16[512,128]{0,1:T(8,128)(2,1)}, bf16[512,128]{0,1:T(8,128)(2,1)}, u32[]{:S(2)}, u32[]{:S(2)}) collective-permute-start(bf16[512,128]{0,1:T(8,128)(2,1)} %collective-permute-done), channel_id=1, source_target_pairs={{0,1},{1,2},{2,3},{3,4},{4,5},{5,6},{6,7},{7,8},{8,9},{9,10},{10,1... | collective-permute-start | bytes 393224 | tf_op jit(solution)/shard_map/ppermute | solution.py:14
  59.9 7.4 %collective-permute-start.4 = (bf16[512,128]{0,1:T(8,128)(2,1)}, bf16[512,128]{0,1:T(8,128)(2,1)}, u32[]{:S(2)}, u32[]{:S(2)}) collective-permute-start(bf16[512,128]{0,1:T(8,128)(2,1)} %collective-permute-done.2), channel_id=1, source_target_pairs={{0,1},{1,2},{2,3},{3,4},{4,5},{5,6},{6,7},{7,8},{8,9},{9,10},{10,1... | collective-permute-start | bytes 393224 | tf_op jit(solution)/shard_map/ppermute | solution.py:14
  84.1 22.4 %collective-permute-start.5 = (f32[16,8]{1,0:T(8,128)}, f32[16,8]{1,0:T(8,128)}, u32[]{:S(2)}, u32[]{:S(2)}) collective-permute-start(f32[16,8]{1,0:T(8,128)} %copy.29), channel_id=1, source_target_pairs={{0,13},{1,14},{2,15},{3,0},{4,1},{5,2},{6,3},{7,4},{8,5},{9,6},{10... | collective-permute-start | bytes 1544 | tf_op jit(solution)/shard_map/ppermute | solution.py:14
  89.8 16.8 %collective-permute-start.1 = (f32[16,8]{1,0:T(8,128)}, f32[16,8]{1,0:T(8,128)}, u32[]{:S(2)}, u32[]{:S(2)}) collective-permute-start(f32[16,8]{1,0:T(8,128)} %copy.27), channel_id=1, source_target_pairs={{0,15},{1,0},{2,1},{3,2},{4,3},{5,4},{6,5},{7,6},{8,7},{9,8},{10,9... | collective-permute-start | bytes 1544 | tf_op jit(solution)/shard_map/ppermute | solution.py:14
  97.4 9.1 %collective-permute-start.3 = (f32[16,8]{1,0:T(8,128)}, f32[16,8]{1,0:T(8,128)}, u32[]{:S(2)}, u32[]{:S(2)}) collective-permute-start(f32[16,8]{1,0:T(8,128)} %copy.28), channel_id=1, source_target_pairs={{0,14},{1,15},{2,0},{3,1},{4,2},{5,3},{6,4},{7,5},{8,6},{9,7},{10,... | collective-permute-start | bytes 1544 | tf_op jit(solution)/shard_map/ppermute | solution.py:14
  109.6 13.0 %collective-permute-start.6 = (f32[16,8]{1,0:T(8,128)}, f32[16,8]{1,0:T(8,128)}, u32[]{:S(2)}, u32[]{:S(2)}) collective-permute-start(f32[16,8]{1,0:T(8,128)} %get-tuple-element.19), channel_id=1, source_target_pairs={{0,1},{1,2},{2,3},{3,4},{4,5},{5,6},{6,7},{7,8},{8,9},{9,10},{10,1... | collective-permute-start | bytes 1544 | tf_op jit(solution)/shard_map/ppermute | solution.py:14
  110.4 20.3 %collective-permute-start.10 = (f32[16,8]{1,0:T(8,128)}, f32[16,8]{1,0:T(8,128)}, u32[]{:S(2)}, u32[]{:S(2)}) collective-permute-start(f32[16,8]{1,0:T(8,128)} %get-tuple-element.17), channel_id=1, source_target_pairs={{0,3},{1,4},{2,5},{3,6},{4,7},{5,8},{6,9},{7,10},{8,11},{9,12},{10... | collective-permute-start | bytes 1544 | tf_op jit(solution)/shard_map/ppermute | solution.py:14
  113.8 13.1 %collective-permute-start.8 = (f32[16,8]{1,0:T(8,128)}, f32[16,8]{1,0:T(8,128)}, u32[]{:S(2)}, u32[]{:S(2)}) collective-permute-start(f32[16,8]{1,0:T(8,128)} %get-tuple-element.18), channel_id=1, source_target_pairs={{0,2},{1,3},{2,4},{3,5},{4,6},{5,7},{6,8},{7,9},{8,10},{9,11},{10,... | collective-permute-start | bytes 1544 | tf_op jit(solution)/shard_map/ppermute | solution.py:14
  141.5 3.1 %copy-start.6 = (f32[512,8]{0,1:T(8,128)S(1)}, f32[512,8]{0,1:T(8,128)}, u32[]{:S(2)}) copy-start(f32[512,8]{0,1:T(8,128)} %div.133) | copy-start | bytes 49156
  146.7 3.1 %copy-start.12 = (pred[1440]{0:T(1024)(128)(4,1)S(1)}, pred[1440]{0:T(1024)(128)(4,1)}, u32[]{:S(2)}) copy-start(pred[1440]{0:T(1024)(128)(4,1)} %lt.42) | copy-start | bytes 4324
  159.7 11.6 %collective-permute-start.9 = (f32[512,128]{0,1:T(8,128)S(1)}, f32[512,128]{0,1:T(8,128)S(1)}, u32[]{:S(2)}, u32[]{:S(2)}) collective-permute-start(f32[512,128]{0,1:T(8,128)S(1)} %fusion.19), channel_id=1, source_target_pairs={{0,14},{1,15},{2,0},{3,1},{4,2},{5,3},{6,4},{7,5},{8,6},{9,7},{10,... | collective-permute-start | bytes 786440 | tf_op jit(solution)/shard_map/ppermute | solution.py:14
  164.5 10.0 %collective-permute-start.7 = (f32[512,128]{0,1:T(8,128)S(1)}, f32[512,128]{0,1:T(8,128)S(1)}, u32[]{:S(2)}, u32[]{:S(2)}) collective-permute-start(f32[512,128]{0,1:T(8,128)S(1)} %fusion.18), channel_id=1, source_target_pairs={{0,15},{1,0},{2,1},{3,2},{4,3},{5,4},{6,5},{7,6},{8,7},{9,8},{10,9... | collective-permute-start | bytes 786440 | tf_op jit(solution)/shard_map/ppermute | solution.py:14
  164.5 12.8 %collective-permute-start.11 = (f32[512,128]{0,1:T(8,128)S(1)}, f32[512,128]{0,1:T(8,128)S(1)}, u32[]{:S(2)}, u32[]{:S(2)}) collective-permute-start(f32[512,128]{0,1:T(8,128)S(1)} %fusion.20), channel_id=1, source_target_pairs={{0,13},{1,14},{2,15},{3,0},{4,1},{5,2},{6,3},{7,4},{8,5},{9,6},{10... | collective-permute-start | bytes 786440 | tf_op jit(solution)/shard_map/ppermute | solution.py:14
  165.0 3.0 %copy-start.2 = (f32[1440,128]{1,0:T(8,128)S(1)}, f32[1440,128]{1,0:T(8,128)}, u32[]{:S(2)}) copy-start(f32[1440,128]{1,0:T(8,128)} %copy-done.1) | copy-start | bytes 2211844
  165.0 3.0 %copy-start.8 = (f32[1440]{0:T(1024)S(1)}, f32[1440]{0:T(1024)}, u32[]{:S(2)}) copy-start(f32[1440]{0:T(1024)} %copy-done.7) | copy-start | bytes 17284
  169.6 7.7 %copy-start.4 = (f32[512,128]{0,1:T(8,128)S(1)}, f32[512,128]{0,1:T(8,128)}, u32[]{:S(2)}) copy-start(f32[512,128]{0,1:T(8,128)} %copy-done.3) | copy-start | bytes 786436
  169.6 7.7 %copy-start.10 = (f32[512]{0:T(512)S(1)}, f32[512]{0:T(512)}, u32[]{:S(2)}) copy-start(f32[512]{0:T(512)} %copy-done.9) | copy-start | bytes 6148
Sparse Core Ops, SparseCore 0:
  179.1 56.0 reduce-scatter.3
where the time goes:
time: 244 us; the launch traced here: 242 us
  local copies, waits for them, and re-layouts  70.7 us (29%)
  waiting for transfers between devices  64.7 us (27%)
  other arithmetic  33.5 us (14%)
  blocking collectives  24.4 us (10%)
  matrix products  21.7 us (9%)
  between operations  14.3 us (6%)
  starting transfers between devices  12.6 us (5%)
    unnamed x2, waiting for transfers between devices  56.2 us
    all_gather x1, blocking collectives, per_device(): stored = lax.all_gather(teacher_rows, 'blk', axis=0, tiled=True)  24.4 us
    mul x8, local copies, waits for them, and re-layouts, score_grads(): natural_power_entries * scale[:, :, None]  20.6 us
    exp x4, local copies, waits for them, and re-layouts, token_terms(): jnp.exp(token_affinity_table / smoothing_heat_factor)  12.6 us
    ppermute x12, starting transfers between devices, shifted(): return lax.ppermute(value, axis, pairs)  12.6 us
    dot_general x4, matrix products, token_terms(): lax.dot_general(query_flat, passage_flat, (((1,), (1,)), ((), ())), prefe...  11.3 us
    div x8, local copies, waits for them, and re-layouts, score_grads(): score_grad[:, None, :] / power_totals_row.reshape(query_matrix, -1, count)  9.58 us
    convert_element_type x1, other arithmetic, score_grads(): (natural_power_entries * scale[:, :, None]).reshape(rows, -1)  8.56 us
  transfers between devices with their start and end apart: 13, of which 6 were waited for; matrix products, arithmetic and copies ran while one was open for 30% of the time, Pallas kernels for 0%

commit v1 on v0

--- a/solution.py
+++ b/solution.py
@@ -1,11 +1,43 @@
+import functools
 import jax
 import jax.numpy as jnp
 from jax import lax
 from jax.sharding import PartitionSpec as P
+from jax.lax import axis_index, ppermute, psum
 
 CYCLE = 4
 smoothing_heat_factor = 0.05
 epsilon = 1e-06
+
+
+def change_lines(obj, axis_no):
+    outer = list(obj.shape[1:])
+    outer[axis_no] *= obj.shape[0]
+    return jnp.moveaxis(obj, 0, axis_no).reshape(outer)
+
+
+def process_waves(arr, shard_axis):
+    current_value = psum(1, axis_name=shard_axis)
+    aux = axis_index(shard_axis)
+    x_next, back = (current_value, aux)
+    e_now, w1 = (arr[None], 1)
+    while w1 < x_next:
+        lanes = []
+        for kk in tuple(range(x_next)):
+            lanes.append((kk, kk ^ w1))
+        block_last = ppermute(e_now, axis_name=shard_axis, perm=lanes)
+        finding = back & w1 == 0
+        next_value = jnp.where(finding, e_now, block_last)
+        e_now = jnp.concatenate([next_value, jnp.where(finding, block_last, e_now)])
+        w1 *= 2
+    return e_now
+
+
+def _work_frames(mine_x, original, d_out):
+    return change_lines(process_waves(mine_x, original), d_out)
+
+
+derive_weights = functools.partial(_work_frames, original="blk", d_out=0)
 
 
 def shifted(value, axis, steps):
@@ -92,7 +124,7 @@
     )
     query_outgoing = query_unit.astype(jnp.bfloat16)
     passage_send = passage_unit.astype(jnp.bfloat16)
-    stored = lax.all_gather(teacher_rows, "blk", axis=0, tiled=True)
+    stored = derive_weights(teacher_rows)
     teacher = jnp.take(stored, teacher_pos, axis=0)
     score_parts = []
     held = []

time: 244 us -> 231 us (0.947)
  blocking collectives: 24.4 us -> 0 us
  starting transfers between devices: 12.6 us -> 20.9 us
  local copies, waits for them, and re-layouts: 70.7 us -> 67.5 us
  other arithmetic: 33.5 us -> 36.6 us
  waiting for transfers between devices: 64.7 us -> 67.5 us
    all_gather x1 -> x0, blocking collectives: 24.4 us -> none  [per_device(): stored = lax.all_gather(teacher_rows, 'blk', axis=0, tiled=True)]
    ppermute x0 -> x4, starting transfers between devices: none -> 7.95 us  [process_waves(): block_last = ppermute(e_now, axis_name=shard_axis, perm=lanes)]
    ppermute x0 -> x4, waiting for transfers between devices: none -> 3.03 us  [process_waves(): block_last = ppermute(e_now, axis_name=shard_axis, perm=lanes)]
    select_n x0 -> x4, other arithmetic: none -> 3.01 us  [process_waves(): next_value = jnp.where(finding, e_now, block_last)]
    concatenate x0 -> x4, other arithmetic: none -> 2.78 us  [process_waves(): e_now = jnp.concatenate([next_value, jnp.where(finding, block_last, e_now)])]
    unnamed x30 -> x36, local copies, waits for them, and re-layouts: 6.97 us -> 7.04 us
  transfers between devices with their start and end apart: 13 -> 17, of which waited for: 6 -> 8; matrix products, arithmetic and copies ran while one was open for 30% -> 32% of each run, Pallas kernels for 0% -> 0%
where the time goes in v1:
time: 231 us; the launch traced here: 229 us
  local copies, waits for them, and re-layouts  67.5 us (29%)
  waiting for transfers between devices  67.5 us (29%)
  other arithmetic  36.6 us (16%)
  matrix products  21.7 us (9%)
  starting transfers between devices  20.9 us (9%)
  between operations  14.4 us (6%)
    unnamed x2, waiting for transfers between devices  56.2 us
    mul x8, local copies, waits for them, and re-layouts, score_grads(): natural_power_entries * scale[:, :, None]  20.6 us
    ppermute x12, starting transfers between devices, shifted(): return lax.ppermute(value, axis, pairs)  12.9 us
    exp x4, local copies, waits for them, and re-layouts, token_terms(): jnp.exp(token_affinity_table / smoothing_heat_factor)  12.6 us
    dot_general x4, matrix products, token_terms(): lax.dot_general(query_flat, passage_flat, (((1,), (1,)), ((), ())), prefe...  11.3 us
    div x8, local copies, waits for them, and re-layouts, score_grads(): score_grad[:, None, :] / power_totals_row.reshape(query_matrix, -1, count)  9.59 us
    convert_element_type x1, other arithmetic, score_grads(): (natural_power_entries * scale[:, :, None]).reshape(rows, -1)  8.56 us
    ppermute x12, waiting for transfers between devices, shifted(): return lax.ppermute(value, axis, pairs)  8.21 us
  transfers between devices with their start and end apart: 17, of which 8 were waited for; matrix products, arithmetic and copies ran while one was open for 32% of the time, Pallas kernels for 0%

profile of v1, /device:TPU:0, one launch (start us, length us, event | category | flops | bytes accessed | tf_op | source)
XLA Modules:
  0.0 228.6 jit_solution(17508070008169376658)
XLA Ops:
  8.3 1.3 multiply_reduce_fusion.3
  10.9 1.3 iota_compare_fusion
  12.2 3.4 %copy.26 = bf16[8,180,768]{2,1,0:T(8,128)(2,1)} copy(bf16[8,180,768]{2,0,1:T(8,128)(2,1)} %param.8) | data formatting | bytes 4423680 | tf_op args[1]
  15.6 2.6 %reshape.166 = bf16[1440,768]{1,0:T(8,128)(2,1)S(1)} reshape(bf16[8,180,768]{2,1,0:T(8,128)(2,1)} %copy.26) | data formatting | bytes 4423680 | tf_op jit(solution)/shard_map/reshape | solution.py:118
  18.2 0.9 multiply_reduce_fusion.1
  19.2 0.8 copy-done.1
  20.3 2.1 fusion
  22.9 2.6 %collective-permute-start.1 = (f32[2,16,32]{2,1,0:T(8,128)S(1)}, f32[2,16,32]{2,1,0:T(8,128)}, u32[]{:S(2)}, u32[]{:S(2)}) collective-permute-start(f32[2,16,32]{2,1,0:T(8,128)S(1)} %pad_maximum_fusion.3), channel_id=1, source_target_pairs={{0,2},{1,3},{2,0},{3,1},{4,6},{5,7},{6,4},{7,5},{8,10},{9,11},{10,... | collective-permute-start | bytes 12296 | tf_op jit(solution)/shard_map/ppermute | solution.py:28
  26.0 1.3 collective-permute-done.1
  28.7 2.1 collective-permute-start.2
  31.5 1.7 collective-permute-done.2
  35.3 2.8 %collective-permute-start.3 = (f32[8,16,32]{2,1,0:T(8,128)}, f32[8,16,32]{2,1,0:T(8,128)}, u32[]{:S(2)}, u32[]{:S(2)}) collective-permute-start(f32[8,16,32]{2,1,0:T(8,128)} %pad_maximum_fusion.1), channel_id=1, source_target_pairs={{0,8},{1,9},{2,10},{3,11},{4,12},{5,13},{6,14},{7,15},{8,0},{9,1},... | collective-permute-start | bytes 49160 | tf_op jit(solution)/shard_map/ppermute | solution.py:28
  38.0 1.3 pad_clamp_fusion
  39.5 3.1 %exp.40 = f32[512,8,180]{0,2,1:T(8,128)} reshape(f32[512,1440]{0,1:T(8,128)} %fusion) | data formatting | bytes 5898240 | tf_op jit(solution)/shard_map/exp | solution.py:64
  43.2 1.5 broadcast_select_fusion.1
  44.7 3.1 %fusion.1 = f32[512,1440]{0,1:T(8,128)} fusion(bf16[1440,128]{1,0:T(8,128)(2,1)S(1)} %fusion.16, bf16[512,128]{0,1:T(8,128)(2,1)} %collective-permute-done.4), kind=kOutput, calls=%fused_computation.6 | convolution fusion | flops 189480960 | bytes 3448832 | tf_op jit(solution)/shard_map/dot_general | solution.py:56
  47.8 3.1 %exp.42 = f32[512,8,180]{0,2,1:T(8,128)} reshape(f32[512,1440]{0,1:T(8,128)} %fusion.1) | data formatting | bytes 5898240 | tf_op jit(solution)/shard_map/exp | solution.py:64
  50.9 1.2 collective-permute-done.6
  52.5 3.1 %fusion.2 = f32[512,1440]{0,1:T(8,128)} fusion(bf16[1440,128]{1,0:T(8,128)(2,1)S(1)} %fusion.16, bf16[512,128]{0,1:T(8,128)(2,1)} %collective-permute-done.6), kind=kOutput, calls=%fused_computation.7 | convolution fusion | flops 189480960 | bytes 3448832 | tf_op jit(solution)/shard_map/dot_general | solution.py:56
  55.6 3.2 %exp.44 = f32[512,8,180]{0,2,1:T(8,128)} reshape(f32[512,1440]{0,1:T(8,128)} %fusion.2) | data formatting | bytes 5898240 | tf_op jit(solution)/shard_map/exp | solution.py:64
  59.5 3.1 %fusion.3 = f32[512,1440]{0,1:T(8,128)} fusion(bf16[1440,128]{1,0:T(8,128)(2,1)S(1)} %fusion.16, bf16[512,128]{0,1:T(8,128)(2,1)} %collective-permute-done.8), kind=kOutput, calls=%fused_computation.8 | convolution fusion | flops 189480960 | bytes 3448832 | tf_op jit(solution)/shard_map/dot_general | solution.py:56
  62.6 3.2 %exp.46 = f32[512,8,180]{0,2,1:T(8,128)} reshape(f32[512,1440]{0,1:T(8,128)} %fusion.3) | data formatting | bytes 5898240 | tf_op jit(solution)/shard_map/exp | solution.py:64
  65.7 5.7 %select_reduce_fusion.3 = (f32[512,8]{0,1:T(8,128)}, f32[512,8]{0,1:T(8,128)S(1)}, f32[512,8]{0,1:T(8,128)S(1)}, f32[512,8]{0,1:T(8,128)S(1)}) fusion(f32[512,8,180]{0,2,1:T(8,128)} %exp.40, pred[8,180]{1,0:T(8,128)(4,1)S(1)} %copy-done.11, f32[512,8,180]{0,2,1:T(8,128)} %exp.42, f32[512,8,180]{0,2,1:T(8,128)} %exp.44, f32[512,8,180]{0,2,1:T(8,128)} %exp.46), kind=kLoop, calls=%fused_computation.12 | loop fusion | flops 5881856 | bytes 11863456 | tf_op jit(solution)/shard_map/reduce_sum | solution.py:66
  72.0 1.4 mul.112
  73.5 0.9 reduce_sum.161
  75.1 0.9 collective-permute-start.9
  75.9 1.3 log_multiply_fusion.2
  77.3 1.4 mul.108
  78.7 0.9 reduce_sum.157
  80.3 2.5 %collective-permute-start.5 = (f32[16,8]{1,0:T(8,128)}, f32[16,8]{1,0:T(8,128)}, u32[]{:S(2)}, u32[]{:S(2)}) collective-permute-start(f32[16,8]{1,0:T(8,128)} %copy.27), channel_id=1, source_target_pairs={{0,15},{1,0},{2,1},{3,2},{4,3},{5,4},{6,5},{7,6},{8,7},{9,8},{10,9... | collective-permute-start | bytes 1544 | tf_op jit(solution)/shard_map/ppermute | solution.py:46
  82.8 1.4 mul.110
  84.2 0.9 reduce_sum.159
  86.3 1.5 pad_maximum_fusion
  87.8 1.6 gather_fusion
  89.4 1.4 mul.106
  90.8 1.5 reduce_sum.155
  92.3 1.3 copy.30
  93.7 1.0 fusion.14
  94.7 1.4 divide_subtract_fusion
  97.4 3.1 %collective-permute-start.14 = (f32[16,8]{1,0:T(8,128)}, f32[16,8]{1,0:T(8,128)}, u32[]{:S(2)}, u32[]{:S(2)}) collective-permute-start(f32[16,8]{1,0:T(8,128)} %get-tuple-element.25), channel_id=1, source_target_pairs={{0,3},{1,4},{2,5},{3,6},{4,7},{5,8},{6,9},{7,10},{8,11},{9,12},{10... | collective-permute-start | bytes 1544 | tf_op jit(solution)/shard_map/ppermute | solution.py:46
  100.5 1.4 div.128
  101.8 1.5 div.129
  104.1 2.0 mul.114
  106.1 3.1 %mul.115 = f32[512,1440]{0,1:T(8,128)} reshape(f32[512,8,180]{0,2,1:T(8,128)} %mul.114) | data formatting | bytes 5898240 | tf_op jit(solution)/shard_map/mul | solution.py:82
  110.7 1.5 div.132
  112.2 1.3 div.133
  115.0 1.5 div.135
  118.7 1.5 div.138
  121.0 2.0 mul.123
  123.0 3.1 %mul.124 = f32[512,1440]{0,1:T(8,128)} reshape(f32[512,8,180]{0,2,1:T(8,128)} %mul.123) | data formatting | bytes 5898240 | tf_op jit(solution)/shard_map/mul | solution.py:82
  126.1 2.0 mul.120
  128.1 3.1 %mul.121 = f32[512,1440]{0,1:T(8,128)} reshape(f32[512,8,180]{0,2,1:T(8,128)} %mul.120) | data formatting | bytes 5898240 | tf_op jit(solution)/shard_map/mul | solution.py:82
  131.3 2.1 mul.117
  133.4 3.1 %mul.118 = f32[512,1440]{0,1:T(8,128)} reshape(f32[512,8,180]{0,2,1:T(8,128)} %mul.117) | data formatting | bytes 5898240 | tf_op jit(solution)/shard_map/mul | solution.py:82
  136.5 8.6 %multiply_convert_fusion = (bf16[512,1440]{0,1:T(8,128)(2,1)S(1)}, bf16[512,1440]{0,1:T(8,128)(2,1)S(1)}, bf16[512,1440]{0,1:T(8,128)(2,1)S(1)}, bf16[512,1440]{0,1:T(8,128)(2,1)S(1)}) fusion(f32[512,1440]{0,1:T(8,128)} %mul.124, f32[512,1440]{0,1:T(8,128)} %fusion.3, pred[1440]{0:T(1024)(128)(4,1)S(1)} %copy-done.15, f32[512,1440]{0,1:T(8,128)} %mul.118, ...), kind=kLoop, calls=%fused_computation.13 | loop fusion | flops 8847360 | bytes 29492640 | tf_op jit(solution)/shard_map/convert_element_type | solution.py:82
  146.3 4.8 %collective-permute-start.13 = (f32[512,128]{0,1:T(8,128)S(1)}, f32[512,128]{0,1:T(8,128)S(1)}, u32[]{:S(2)}, u32[]{:S(2)}) collective-permute-start(f32[512,128]{0,1:T(8,128)S(1)} %fusion.19), channel_id=1, source_target_pairs={{0,14},{1,15},{2,0},{3,1},{4,2},{5,3},{6,4},{7,5},{8,6},{9,7},{10,... | collective-permute-start | bytes 786440 | tf_op jit(solution)/shard_map/ppermute | solution.py:46
  151.9 1.5 convolution_add_fusion.2
  153.4 1.4 convolution_add_fusion.1
  154.9 1.6 multiply_reduce_fusion
  156.4 1.1 fusion.7
  157.8 3.2 %collective-permute-done.11 = f32[512,128]{0,1:T(8,128)S(1)} collective-permute-done((f32[512,128]{0,1:T(8,128)S(1)}, f32[512,128]{0,1:T(8,128)S(1)}, u32[]{:S(2)}, u32[]{:S(2)}) %collective-permute-start.11) | collective-permute-done | bytes 262176 | tf_op jit(solution)/shard_map/ppermute | solution.py:46
  161.1 2.8 %collective-permute-done.15 = f32[512,128]{0,1:T(8,128)S(1)} collective-permute-done((f32[512,128]{0,1:T(8,128)S(1)}, f32[512,128]{0,1:T(8,128)S(1)}, u32[]{:S(2)}, u32[]{:S(2)}) %collective-permute-start.15) | collective-permute-done | bytes 262176 | tf_op jit(solution)/shard_map/ppermute | solution.py:46
  164.6 0.9 copy.42
  165.6 56.2 %reduce-scatter.4.cloned.1.call-done = f32[48,128]{1,0:T(8,128)} async-done(((f32[768,128]{1,0:T(8,128)}), f32[48,128]{1,0:T(8,128)}) %reduce-scatter.4.cloned.1.call-update) | async-done | bytes 24592
  (95 shorter events, 23.8 us)
Async XLA Ops:
  7.2 1.1 copy-start
  7.2 214.6 %reduce-scatter.4.cloned.1.call-start = ((), (), s32[]{:S(2)}) async-start(), calls=%async_computation.1 | async-start | bytes 417792
  7.2 15.7 %collective-permute-start = (f32[1,16,32]{2,1,0:T(8,128)}, f32[1,16,32]{2,1,0:T(8,128)S(1)}, u32[]{:S(2)}, u32[]{:S(2)}) collective-permute-start(f32[1,16,32]{2,1,0:T(8,128)} %bitcast.73), channel_id=1, source_target_pairs={{0,1},{1,0},{2,3},{3,2},{4,5},{5,4},{6,7},{7,6},{8,9},{9,8},{10,11... | collective-permute-start | bytes 6152 | tf_op jit(solution)/shard_map/ppermute | solution.py:28
  9.6 0.7 copy-start.3
  9.7 0.7 copy-start.12
  10.4 34.3 %collective-permute-start.4 = (bf16[512,128]{0,1:T(8,128)(2,1)S(1)}, bf16[512,128]{0,1:T(8,128)(2,1)}, u32[]{:S(2)}, u32[]{:S(2)}) collective-permute-start(bf16[512,128]{0,1:T(8,128)(2,1)S(1)} %fusion.15), channel_id=1, source_target_pairs={{0,1},{1,2},{2,3},{3,4},{4,5},{5,6},{6,7},{7,8},{8,9},{9,10},{10,1... | collective-permute-start | bytes 393224 | tf_op jit(solution)/shard_map/ppermute | solution.py:46
  15.6 2.6 %copy-start.5 = (bf16[768,128]{1,0:T(8,128)(2,1)S(1)}, bf16[768,128]{1,0:T(8,128)(2,1)}, u32[]{:S(2)}) copy-start(bf16[768,128]{1,0:T(8,128)(2,1)} %param.9) | copy-start | bytes 589828
  19.1 0.9 copy-start.1
  19.1 3.3 %copy-start.16 = (s32[16]{0:T(128)S(1)}, s32[16]{0:T(128)}, u32[]{:S(2)}) copy-start(s32[16]{0:T(128)} %param.11) | copy-start | bytes 196
  19.1 3.8 %copy-start.14 = (f32[16,32]{1,0:T(8,128)S(1)}, f32[16,32]{1,0:T(8,128)}, u32[]{:S(2)}) copy-start(f32[16,32]{1,0:T(8,128)} %param.10) | copy-start | bytes 6148
  19.1 1.1 copy-start.9
  22.9 4.4 %collective-permute-start.1 = (f32[2,16,32]{2,1,0:T(8,128)S(1)}, f32[2,16,32]{2,1,0:T(8,128)}, u32[]{:S(2)}, u32[]{:S(2)}) collective-permute-start(f32[2,16,32]{2,1,0:T(8,128)S(1)} %pad_maximum_fusion.3), channel_id=1, source_target_pairs={{0,2},{1,3},{2,0},{3,1},{4,6},{5,7},{6,4},{7,5},{8,10},{9,11},{10,... | collective-permute-start | bytes 12296 | tf_op jit(solution)/shard_map/ppermute | solution.py:28
  28.1 3.5 %copy-start.7 = (f32[2,16,32]{2,1,0:T(8,128)}, f32[2,16,32]{2,1,0:T(8,128)S(1)}, u32[]{:S(2)}) copy-start(f32[2,16,32]{2,1,0:T(8,128)S(1)} %get-tuple-element.20) | copy-start | bytes 12292
  28.7 4.6 %collective-permute-start.2 = (f32[4,16,32]{2,1,0:T(8,128)}, f32[4,16,32]{2,1,0:T(8,128)}, u32[]{:S(2)}, u32[]{:S(2)}) collective-permute-start(f32[4,16,32]{2,1,0:T(8,128)} %pad_maximum_fusion.2), channel_id=1, source_target_pairs={{0,4},{1,5},{2,6},{3,7},{4,0},{5,1},{6,2},{7,3},{8,12},{9,13},{10,... | collective-permute-start | bytes 24584 | tf_op jit(solution)/shard_map/ppermute | solution.py:28
  34.0 0.6 copy-start.6
  35.3 7.9 %collective-permute-start.3 = (f32[8,16,32]{2,1,0:T(8,128)}, f32[8,16,32]{2,1,0:T(8,128)}, u32[]{:S(2)}, u32[]{:S(2)}) collective-permute-start(f32[8,16,32]{2,1,0:T(8,128)} %pad_maximum_fusion.1), channel_id=1, source_target_pairs={{0,8},{1,9},{2,10},{3,11},{4,12},{5,13},{6,14},{7,15},{8,0},{9,1},... | collective-permute-start | bytes 49160 | tf_op jit(solution)/shard_map/ppermute | solution.py:28
  44.7 7.4 %collective-permute-start.6 = (bf16[512,128]{0,1:T(8,128)(2,1)}, bf16[512,128]{0,1:T(8,128)(2,1)}, u32[]{:S(2)}, u32[]{:S(2)}) collective-permute-start(bf16[512,128]{0,1:T(8,128)(2,1)} %collective-permute-done.4), channel_id=1, source_target_pairs={{0,1},{1,2},{2,3},{3,4},{4,5},{5,6},{6,7},{7,8},{8,9},{9,10},{10,1... | collective-permute-start | bytes 393224 | tf_op jit(solution)/shard_map/ppermute | solution.py:46
  52.1 7.4 %collective-permute-start.8 = (bf16[512,128]{0,1:T(8,128)(2,1)}, bf16[512,128]{0,1:T(8,128)(2,1)}, u32[]{:S(2)}, u32[]{:S(2)}) collective-permute-start(bf16[512,128]{0,1:T(8,128)(2,1)} %collective-permute-done.6), channel_id=1, source_target_pairs={{0,1},{1,2},{2,3},{3,4},{4,5},{5,6},{6,7},{7,8},{8,9},{9,10},{10,1... | collective-permute-start | bytes 393224 | tf_op jit(solution)/shard_map/ppermute | solution.py:46
  62.6 3.2 %copy-start.11 = (pred[8,180]{1,0:T(8,128)(4,1)S(1)}, pred[8,180]{1,0:T(8,128)(4,1)}, u32[]{:S(2)}) copy-start(pred[8,180]{1,0:T(8,128)(4,1)} %iota_compare_fusion) | copy-start | bytes 4324
  75.1 18.6 %collective-permute-start.9 = (f32[16,8]{1,0:T(8,128)}, f32[16,8]{1,0:T(8,128)}, u32[]{:S(2)}, u32[]{:S(2)}) collective-permute-start(f32[16,8]{1,0:T(8,128)} %copy.29), channel_id=1, source_target_pairs={{0,13},{1,14},{2,15},{3,0},{4,1},{5,2},{6,3},{7,4},{8,5},{9,6},{10... | collective-permute-start | bytes 1544 | tf_op jit(solution)/shard_map/ppermute | solution.py:46
  80.3 13.4 %collective-permute-start.5 = (f32[16,8]{1,0:T(8,128)}, f32[16,8]{1,0:T(8,128)}, u32[]{:S(2)}, u32[]{:S(2)}) collective-permute-start(f32[16,8]{1,0:T(8,128)} %copy.27), channel_id=1, source_target_pairs={{0,15},{1,0},{2,1},{3,2},{4,3},{5,4},{6,5},{7,6},{8,7},{9,8},{10,9... | collective-permute-start | bytes 1544 | tf_op jit(solution)/shard_map/ppermute | solution.py:46
  85.8 7.9 %collective-permute-start.7 = (f32[16,8]{1,0:T(8,128)}, f32[16,8]{1,0:T(8,128)}, u32[]{:S(2)}, u32[]{:S(2)}) collective-permute-start(f32[16,8]{1,0:T(8,128)} %copy.28), channel_id=1, source_target_pairs={{0,14},{1,15},{2,0},{3,1},{4,2},{5,3},{6,4},{7,5},{8,6},{9,7},{10,... | collective-permute-start | bytes 1544 | tf_op jit(solution)/shard_map/ppermute | solution.py:46
  96.7 12.5 %collective-permute-start.10 = (f32[16,8]{1,0:T(8,128)}, f32[16,8]{1,0:T(8,128)}, u32[]{:S(2)}, u32[]{:S(2)}) collective-permute-start(f32[16,8]{1,0:T(8,128)} %get-tuple-element.27), channel_id=1, source_target_pairs={{0,1},{1,2},{2,3},{3,4},{4,5},{5,6},{6,7},{7,8},{8,9},{9,10},{10,1... | collective-permute-start | bytes 1544 | tf_op jit(solution)/shard_map/ppermute | solution.py:46
  97.4 19.9 %collective-permute-start.14 = (f32[16,8]{1,0:T(8,128)}, f32[16,8]{1,0:T(8,128)}, u32[]{:S(2)}, u32[]{:S(2)}) collective-permute-start(f32[16,8]{1,0:T(8,128)} %get-tuple-element.25), channel_id=1, source_target_pairs={{0,3},{1,4},{2,5},{3,6},{4,7},{5,8},{6,9},{7,10},{8,11},{9,12},{10... | collective-permute-start | bytes 1544 | tf_op jit(solution)/shard_map/ppermute | solution.py:46
  100.5 13.1 %collective-permute-start.12 = (f32[16,8]{1,0:T(8,128)}, f32[16,8]{1,0:T(8,128)}, u32[]{:S(2)}, u32[]{:S(2)}) collective-permute-start(f32[16,8]{1,0:T(8,128)} %get-tuple-element.26), channel_id=1, source_target_pairs={{0,2},{1,3},{2,4},{3,5},{4,6},{5,7},{6,8},{7,9},{8,10},{9,11},{10,... | collective-permute-start | bytes 1544 | tf_op jit(solution)/shard_map/ppermute | solution.py:46
  128.1 3.1 %copy-start.8 = (f32[512,8]{0,1:T(8,128)S(1)}, f32[512,8]{0,1:T(8,128)}, u32[]{:S(2)}) copy-start(f32[512,8]{0,1:T(8,128)} %div.133) | copy-start | bytes 49156
  133.3 3.1 %copy-start.15 = (pred[1440]{0:T(1024)(128)(4,1)S(1)}, pred[1440]{0:T(1024)(128)(4,1)}, u32[]{:S(2)}) copy-start(pred[1440]{0:T(1024)(128)(4,1)} %lt.42) | copy-start | bytes 4324
  146.3 11.5 %collective-permute-start.13 = (f32[512,128]{0,1:T(8,128)S(1)}, f32[512,128]{0,1:T(8,128)S(1)}, u32[]{:S(2)}, u32[]{:S(2)}) collective-permute-start(f32[512,128]{0,1:T(8,128)S(1)} %fusion.19), channel_id=1, source_target_pairs={{0,14},{1,15},{2,0},{3,1},{4,2},{5,3},{6,4},{7,5},{8,6},{9,7},{10,... | collective-permute-start | bytes 786440 | tf_op jit(solution)/shard_map/ppermute | solution.py:46
  151.1 10.0 %collective-permute-start.11 = (f32[512,128]{0,1:T(8,128)S(1)}, f32[512,128]{0,1:T(8,128)S(1)}, u32[]{:S(2)}, u32[]{:S(2)}) collective-permute-start(f32[512,128]{0,1:T(8,128)S(1)} %fusion.18), channel_id=1, source_target_pairs={{0,15},{1,0},{2,1},{3,2},{4,3},{5,4},{6,5},{7,6},{8,7},{9,8},{10,9... | collective-permute-start | bytes 786440 | tf_op jit(solution)/shard_map/ppermute | solution.py:46
  151.1 12.8 %collective-permute-start.15 = (f32[512,128]{0,1:T(8,128)S(1)}, f32[512,128]{0,1:T(8,128)S(1)}, u32[]{:S(2)}, u32[]{:S(2)}) collective-permute-start(f32[512,128]{0,1:T(8,128)S(1)} %fusion.20), channel_id=1, source_target_pairs={{0,13},{1,14},{2,15},{3,0},{4,1},{5,2},{6,3},{7,4},{8,5},{9,6},{10... | collective-permute-start | bytes 786440 | tf_op jit(solution)/shard_map/ppermute | solution.py:46
  151.9 3.0 %copy-start.2 = (f32[1440,128]{1,0:T(8,128)S(1)}, f32[1440,128]{1,0:T(8,128)}, u32[]{:S(2)}) copy-start(f32[1440,128]{1,0:T(8,128)} %copy-done.1) | copy-start | bytes 2211844
  151.9 3.0 %copy-start.10 = (f32[1440]{0:T(1024)S(1)}, f32[1440]{0:T(1024)}, u32[]{:S(2)}) copy-start(f32[1440]{0:T(1024)} %copy-done.9) | copy-start | bytes 17284
  156.4 7.5 %copy-start.4 = (f32[512,128]{0,1:T(8,128)S(1)}, f32[512,128]{0,1:T(8,128)}, u32[]{:S(2)}) copy-start(f32[512,128]{0,1:T(8,128)} %copy-done.3) | copy-start | bytes 786436
  156.4 7.5 %copy-start.13 = (f32[512]{0:T(512)S(1)}, f32[512]{0:T(512)}, u32[]{:S(2)}) copy-start(f32[512]{0:T(512)} %copy-done.12) | copy-start | bytes 6148
Sparse Core Ops, SparseCore 0:
  165.7 56.0 reduce-scatter.3
